TPU v7x, 512 devices: a whole 4x4x16 slice. The times are simulated.
512 devices in a mesh: dp: 32 (over y, x, core), seq: 16 (over z).
Axes of the slice: x: 4, y: 4, z: 16, core: 2. Of those that a mesh axis runs over, the one named last changes fastest.
Arguments:
- loader_rows: bfloat16 [3, 32, 1280, 4096], P(None, 'dp', 'seq'), may hold values from -6 to 6
- cotangent: bfloat16 [32, 1280, 4096], P('dp', None, 'seq'), may hold values from -6 to 6
- gains: float32 [2, 32, 128], P(None, 'seq'), may hold values from 0.25 to 1.75
- block_rows: int32 [32, 16, 32], replicated, may hold values from 0 to 3, as said below
- block_clip: int32 [32, 32], replicated, may hold values from 0 to 3
Outputs:
- gradients: bfloat16 [3, 32, 1280, 4096], P(None, 'dp', 'seq')
- gain_grads: float32 [2, 32, 128], P(None, 'seq')
Inputs may be any that keep to these rules, and one draw needn't show every extreme that they name: `block_rows`: in every sequence shard, each loader shard sends at most 80 rows in all and each pack receives at most 80 rows in all; some loader shard sends and some pack receives exactly 80, and some block has exactly 3 rows.
All inputs are finite; a program needn't handle non-finite values.
Results may differ from a plain program's by a relative error of at most 0.0071.
Values may be sent and summed in bfloat16 or wider, within the bound.
No kernel may reach another device: no remote copies, remote signals or barrier semaphores. Data moves between devices by JAX's collectives and lax.ppermute only.
A program may use at most 64 MiB of HBM per device.

v0:
```python
import functools
import math

import jax
import jax.numpy as jnp
from jax import lax
from jax.experimental import pallas as pl
from jax.experimental.pallas import tpu as pltpu
from jax.sharding import PartitionSpec as P


epsilon = 1e-06
SLOTS = 3
EXTRA = 8
GROUP = 8


def iota(shape, axis):
    return lax.broadcasted_iota(jnp.int32, shape, axis)


def dot(left, right, left_axis=1, right_axis=0):
    return lax.dot_general(
        left,
        right,
        (((left_axis,), (right_axis,)), ((), ())),
        preferred_element_type=jnp.float32,
    )


def gather_kernel(
    loaders, bands, capacity,
    place_ref, table_ref, rows_ref, own_ref, other_ref, pick_ref, pick_last_ref, last_ref,
):
    step = pl.program_id(0)
    steps = pl.num_programs(0)
    lines = loaders * GROUP
    half = rows_ref.shape[1] // 2
    me = place_ref[0]

    @pl.when(step == 0)
    def _():
        my_loader = me // bands
        my_core = my_loader % 2
        column = iota((1, loaders * bands), 1)
        band = column % bands
        target = jnp.where(band == me % bands, column // bands, -1)
        owner = iota((loaders, 1), 0)
        owner = 2 * (owner % (loaders // 2)) + (owner // (loaders // 2) + my_core) % 2
        before = jnp.where((target < owner) & (target >= 0), 1.0, 0.0)
        same = jnp.where(target == owner, 1.0, 0.0)
        table = table_ref[...].astype(jnp.float32).astype(jnp.bfloat16)
        sums = dot(jnp.concatenate([before, same], axis=0).astype(jnp.bfloat16), table)
        sums = jnp.where(iota(sums.shape, 1) == my_loader, sums, 0.0)
        sums = jnp.sum(sums, axis=1, keepdims=True)
        start, count = sums[:loaders].astype(jnp.int32), sums[loaders:].astype(jnp.int32)
        last_column = jnp.where(count > SLOTS - 1, start + (SLOTS - 1), -1)
        pick_last_ref[...] = jnp.where(iota((loaders, capacity), 1) == last_column, 1.0, 0.0).astype(jnp.bfloat16)
        spread = jnp.where(iota((lines, 1), 0) // GROUP == iota((1, loaders), 1), 1.0, 0.0).astype(jnp.bfloat16)
        wide = dot(spread, jnp.concatenate([start, count], axis=1).astype(jnp.float32).astype(jnp.bfloat16))
        start, count = wide[:, 0:1].astype(jnp.int32), wide[:, 1:2].astype(jnp.int32)
        kind = iota((lines, 1), 0) % GROUP
        slot = kind // 3
        line_column = jnp.where(slot < count, (kind - 3 * slot) * capacity + start + slot, -1)
        lanes = iota((lines, 3 * capacity), 1)
        pick_ref[...] = jnp.where(lanes == line_column, 1.0, 0.0).astype(jnp.bfloat16)

    @pl.when(step < steps - 1)
    def _():
        picked = dot(pick_ref[...], rows_ref[...]).astype(jnp.bfloat16)
        own_ref[...] = picked[: lines // 2]
        other_ref[...] = picked[lines // 2 :]
        last = dot(pick_last_ref[...], rows_ref[2 * capacity :])
        for part in range(2):
            group = (2 * step + part) % GROUP
            for low in range(0, half, 128):
                tile = (2 * step // GROUP) * (half // 128) + low // 128
                at = part * half + low
                last_ref[tile, pl.ds(group, loaders, stride=GROUP), :] = last[:, at : at + 128]

    @pl.when(step == steps - 1)
    def _():
        for tile in range(last_ref.shape[0]):
            at = slice(tile * 128, (tile + 1) * 128)
            last = last_ref[tile].astype(jnp.bfloat16)
            own_ref[:, at] = last[: lines // 2]
            other_ref[:, at] = last[lines // 2 :]


def chunk_kernel(capacity, cot_ref, gains_ref, out_ref):
    gains = gains_ref[...]
    row = iota((EXTRA, 2 * gains.shape[2]), 0)
    extra = jnp.zeros(row.shape, jnp.float32)
    for kind in range(2):
        line = jnp.concatenate([gains[kind, 0:1], gains[kind, 1:2]], axis=1)
        for part in range(3):
            piece = line.astype(jnp.bfloat16).astype(jnp.float32)
            extra = jnp.where(row == 2 * part + kind, piece, extra)
            line = line - piece
    extra = extra.astype(jnp.bfloat16)
    for chunk in range(cot_ref.shape[0]):
        out_ref[chunk, :capacity] = cot_ref[chunk]
        out_ref[chunk, capacity:] = extra


def attention_kernel(
    loaders, bands, capacity, head_size,
    place_ref, table_ref, clip_ref, rows_ref, last_rows_ref, chunk_ref,
    grad_ref, gain_ref,
    pick_ref, pick_last_ref, same_ref,
):
    step = pl.program_id(0)
    lines = loaders * GROUP
    scale = 1.0 / math.sqrt(head_size)
    me = place_ref[0]
    my_core = (me // bands) % 2
    table_row = table_ref[pl.ds(me, 1), :]
    total = jnp.sum(table_row, axis=1, keepdims=True)
    valid = iota((capacity, 1), 0) < total

    @pl.when(step == 0)
    def _():
        counts = jnp.broadcast_to(table_row, (8, loaders)).astype(jnp.float32).astype(jnp.bfloat16)
        block = iota((loaders, lines), 1) // GROUP
        source = block - block % 2 + (block % 2 + my_core) % 2
        entry = iota((loaders, lines), 0)
        start = dot(counts, jnp.where(entry < source, 1.0, 0.0).astype(jnp.bfloat16))[:1].astype(jnp.int32)
        count = dot(counts, jnp.where(entry == source, 1.0, 0.0).astype(jnp.bfloat16))[:1].astype(jnp.int32)
        kind = iota((1, lines), 1) % GROUP
        slot = kind // 3
        place = iota((capacity, lines), 0)
        hit = (place == start + slot) & (slot < count)
        for part in range(3):
            pick_ref[part * capacity : (part + 1) * capacity] = jnp.where(
                hit & (kind % 3 == part), 1.0, 0.0
            ).astype(jnp.bfloat16)
        hit_last = (place == start + (SLOTS - 1)) & (count > SLOTS - 1)
        pick_last_ref[...] = jnp.where(hit_last, 1.0, 0.0).astype(jnp.bfloat16)
        clip_row = clip_ref[pl.ds(me // bands, 1), :]
        clip_lines = dot(
            jnp.broadcast_to(clip_row, (8, loaders)).astype(jnp.float32).astype(jnp.bfloat16),
            jnp.where(entry == source, 1.0, 0.0).astype(jnp.bfloat16),
        )[:1].astype(jnp.int32)
        first = kind == 0
        owned = (place >= start) & (place < start + count) & first
        owned = jnp.where(owned, 1.0, 0.0).astype(jnp.bfloat16)
        label_is = jnp.where(iota((16, lines), 0) == clip_lines, 1.0, 0.0).astype(jnp.bfloat16)
        label = dot(owned, label_is, 1, 1)
        label = jnp.where(iota((capacity, 16), 1) == 15, jnp.where(valid, 0.0, 1.0), label)
        label = label.astype(jnp.bfloat16)
        same_ref[...] = dot(label, label, 1, 1)

    same = same_ref[...] > 0.5
    group = iota((capacity, lines), 1) % GROUP
    width = 2 * head_size
    heads = [slice(head * head_size, (head + 1) * head_size) for head in range(2)]
    in_head = iota((width, width), 0) // head_size == iota((width, width), 1) // head_size
    averager = jnp.where(in_head, 1.0 / head_size, 0.0).astype(jnp.bfloat16)
    bfloat = jnp.bfloat16

    def average(rows):
        return dot(rows, averager)

    units = chunk_ref.shape[0]
    pick_last = [
        jnp.where(group == (units * step + unit) % GROUP, pick_last_ref[...], jnp.zeros((), bfloat))
        for unit in range(units)
    ]
    packed = dot(pick_ref[...], rows_ref[...])
    last = dot(jnp.concatenate(pick_last, axis=0), last_rows_ref[...])
    lane = [slice(unit * width, (unit + 1) * width) for unit in range(units)]
    span = [slice(unit * capacity, (unit + 1) * capacity) for unit in range(units)]
    value = [(packed[2 * capacity :, lane[u]] + last[span[u]]).astype(bfloat) for u in range(units)]
    extra = [chunk_ref[u, capacity:].astype(jnp.float32) for u in range(units)]
    gains = [rows[0:2] + rows[2:4] + rows[4:6] for rows in extra]
    dout = [jnp.where(valid, chunk_ref[u, :capacity], jnp.zeros((), bfloat)) for u in range(units)]
    raw = jnp.concatenate(
        [packed[part * capacity : (part + 1) * capacity, lane[u]] for part in range(2) for u in range(units)], axis=0
    )
    centred = raw - average(raw.astype(bfloat))
    factor = lax.rsqrt(average((centred * centred).astype(bfloat)) + epsilon)
    hat = centred * factor
    hats = [[hat[(part * units + u) * capacity :][:capacity] for u in range(units)] for part in range(2)]
    qn = [(hats[0][u] * gains[u][0:1]).astype(bfloat) for u in range(units)]
    kn = [(hats[1][u] * gains[u][1:2]).astype(bfloat) for u in range(units)]
    each = [(u, lanes) for u in range(units) for lanes in heads]
    score = [dot(kn[u][:, lanes], qn[u][:, lanes], 1, 1) for u, lanes in each]
    dprob = [dot(value[u][:, lanes], dout[u][:, lanes], 1, 1) for u, lanes in each]
    weight = [jnp.where(same, jnp.exp(rows * scale), 0.0) for rows in score]
    prob = [rows * (1.0 / jnp.sum(rows, axis=0, keepdims=True)) for rows in weight]
    delta = [jnp.sum(p * d, axis=0, keepdims=True) for p, d in zip(prob, dprob)]
    dscore = [(p * (d - e)).astype(bfloat) for p, d, e in zip(prob, dprob, delta)]
    grads = [
        [dot(dscore[n], kn[u][:, lanes], 0, 0) for n, (u, lanes) in enumerate(each)],
        [dot(dscore[n], qn[u][:, lanes]) for n, (u, lanes) in enumerate(each)],
    ]
    dvalue = [dot(prob[n].astype(bfloat), dout[u][:, lanes]) for n, (u, lanes) in enumerate(each)]
    for n, (u, lanes) in enumerate(each):
        grad_ref[2, :, u * width + lanes.start : u * width + lanes.stop] = dvalue[n].astype(bfloat)
    scaled, seconds = [], []
    for part in range(2):
        for u in range(units):
            grad = jnp.concatenate(grads[part][2 * u : 2 * u + 2], axis=1)
            gain = gains[u][part : part + 1] * scale
            product = grad * hats[part][u]
            total_gain = jnp.sum(product, axis=0, keepdims=True) * scale
            for head, lanes in enumerate(heads):
                gain_ref[u, 2 * part + head : 2 * part + head + 1, :] = total_gain[:, lanes]
            scaled.append(grad * gain)
            seconds.append(product * gain)
    scaled = jnp.concatenate(scaled, axis=0)
    first = average(scaled.astype(bfloat))
    second = average(jnp.concatenate(seconds, axis=0).astype(bfloat))
    result = (factor * (scaled - first - hat * second)).astype(bfloat)
    for part in range(2):
        for u in range(units):
            grad_ref[part, :, lane[u]] = result[(part * units + u) * capacity :][:capacity]


def shards(loader_rows, cotangent, gains, block_rows, block_clip):
    loaders = lax.axis_size("chip") * 2
    bands = lax.axis_size("seq")
    capacity = loader_rows.shape[2]
    width = loader_rows.shape[3]
    head_size = gains.shape[2]
    lines = loaders * GROUP
    pair = 2 * head_size
    pairs = width // pair
    place = lax.axis_index(("chip", "core", "seq")).astype(jnp.int32).reshape(1)
    table = block_rows.reshape(loaders * bands, loaders)
    smem = pl.BlockSpec(memory_space=pltpu.SMEM)

    gather = pl.pallas_call(
        functools.partial(gather_kernel, loaders, bands, capacity),
        grid=(width // (2 * pair) + 1,),
        in_specs=[
            smem,
            pl.BlockSpec((loaders * bands, loaders), lambda t: (0, 0)),
            pl.BlockSpec((3 * capacity, 2 * pair), lambda t: (0, jnp.minimum(t, width // (2 * pair) - 1))),
        ],
        out_specs=[pl.BlockSpec((lines // 2, 2 * pair), lambda t: (0, t))] * 2,
        out_shape=[jax.ShapeDtypeStruct((lines // 2, width + 2 * pair), jnp.bfloat16)] * 2,
        scratch_shapes=[
            pltpu.VMEM((lines, 3 * capacity), jnp.bfloat16),
            pltpu.VMEM((loaders, capacity), jnp.bfloat16),
            pltpu.VMEM((2 * pair // 128, lines, 128), jnp.float32),
        ],
        name="gather_rows",
    )
    pack = pl.pallas_call(
        functools.partial(chunk_kernel, capacity),
        grid=(4,),
        in_specs=[
            pl.BlockSpec((bands // 4, capacity, pair), lambda t: (t, 0, 0)),
            pl.BlockSpec((2, 2, head_size), lambda t: (0, 0, 0)),
        ],
        out_specs=pl.BlockSpec((bands // 4, capacity + EXTRA, pair), lambda t: (t, 0, 0)),
        out_shape=jax.ShapeDtypeStruct((bands, capacity + EXTRA, pair), jnp.bfloat16),
        name="chunk_cotangent",
    )
    chunks = pack(cotangent.reshape(bands, capacity, pair), gains)
    own, other = gather(place, table, loader_rows.reshape(3 * capacity, width))
    other = lax.ppermute(other, "core", [(0, 1), (1, 0)])
    shape = (loaders // 2, 1, GROUP, width + 2 * pair)
    outgoing = jnp.concatenate([own.reshape(shape), other.reshape(shape)], axis=1)

    def move_rows(rows):
        return lax.all_to_all(rows, "chip", split_axis=0, concat_axis=0, tiled=True)

    def move_chunks(chunks):
        return lax.all_to_all(chunks, "seq", split_axis=0, concat_axis=0, tiled=True)

    def rows_first(rows, chunks):
        rows, chunks = lax.optimization_barrier((move_rows(rows), chunks))
        return rows, move_chunks(chunks)

    def chunks_first(rows, chunks):
        rows, chunks = lax.optimization_barrier((rows, move_chunks(chunks)))
        return move_rows(rows), chunks

    arrived, chunks = lax.cond(lax.axis_index("core") == 0, rows_first, chunks_first, outgoing, chunks)
    arrived = arrived.reshape(lines, width + 2 * pair)

    attend = pl.pallas_call(
        functools.partial(attention_kernel, loaders, bands, capacity, head_size),
        grid=(pairs // 4,),
        in_specs=[
            smem,
            pl.BlockSpec((loaders * bands, loaders), lambda t: (0, 0)),
            pl.BlockSpec((loaders, loaders), lambda t: (0, 0)),
            pl.BlockSpec((lines, 4 * pair), lambda t: (0, t)),
            pl.BlockSpec((lines, pair), lambda t: (0, pairs + 4 * t // GROUP)),
            pl.BlockSpec((4, capacity + EXTRA, pair), lambda t: (t, 0, 0)),
        ],
        out_specs=[
            pl.BlockSpec((3, capacity, 4 * pair), lambda t: (0, 0, t)),
            pl.BlockSpec((4, 4, head_size), lambda t: (t, 0, 0)),
        ],
        out_shape=[
            jax.ShapeDtypeStruct((3, capacity, width), jnp.bfloat16),
            jax.ShapeDtypeStruct((bands, 4, head_size), jnp.float32),
        ],
        scratch_shapes=[
            pltpu.VMEM((3 * capacity, lines), jnp.bfloat16),
            pltpu.VMEM((capacity, lines), jnp.bfloat16),
            pltpu.VMEM((capacity, capacity), jnp.float32),
        ],
        compiler_params=pltpu.CompilerParams(vmem_limit_bytes=16 << 20),
        name="attend_pack",
    )
    gradients, gain_parts = attend(place, table, block_clip, arrived, arrived, chunks)
    by_head = lax.all_to_all(gain_parts, "seq", split_axis=0, concat_axis=0, tiled=True)
    mine = jnp.sum(by_head, axis=0, keepdims=True)
    every = lax.all_to_all(
        jnp.broadcast_to(mine, (loaders, 4, head_size)), ("chip", "core"), split_axis=0, concat_axis=0, tiled=True
    )
    gain_total = jnp.sum(every, axis=0).reshape(2, 2, head_size)
    return (gradients[:, None], gain_total)


def solution(mesh):
    chips, bands = mesh.devices.shape[0] // 2, mesh.devices.shape[1]
    mesh = jax.sharding.Mesh(mesh.devices.reshape(chips, 2, bands), ("chip", "core", "seq"))
    dp = ("chip", "core")
    in_specs = (P(None, dp, "seq", None), P(dp, None, "seq"), P(None, "seq", None), P(), P())
    out_specs = (P(None, dp, "seq", None), P(None, "seq", None))
    return jax.shard_map(shards, mesh=mesh, in_specs=in_specs, out_specs=out_specs, check_vma=False)
```

profile of v0, /device:TPU:1, one launch (start us, length us, event | category | flops | bytes accessed | tf_op | source)
XLA Modules:
  0.0 120.5 jit_solution(11787989077135369843)
XLA Ops:
  0.6 7.3 %gather_rows.1 = (bf16[128,4608]{1,0:T(8,128)(2,1)}, bf16[128,4608]{1,0:T(8,128)(2,1)}) custom-call(s32[1]{0:T(128)} %bitcast.2.place_ref, s32[512,32]{1,0:T(8,128)} %bitcast.16, bf16[240,4096]{1,0:T(8,128)(2,1)} %bitcast.20), custom_call_target="tpu_custom_call" | custom-call | tf_op jit(solution)/shard_map/gather_rows/pallas_call | solution.py:262
  7.9 8.7 %collective-permute-start = (bf16[128,4608]{1,0:T(8,128)(2,1)}, bf16[128,4608]{1,0:T(8,128)(2,1)S(1)}, u32[]{:S(2)}, u32[]{:S(2)}) collective-permute-start(bf16[128,4608]{1,0:T(8,128)(2,1)} %get-tuple-element.26), channel_id=1, source_target_pairs={{0,16},{16,0},{1,17},{17,1},{2,18},{18,2},{3,19},{19,3},{4,20},{20... | collective-permute-start | bytes 3538952 | tf_op jit(solution)/shard_map/ppermute | solution.py:263
  16.7 2.0 %chunk_cotangent.1 = bf16[16,88,256]{2,1,0:T(8,128)(2,1)S(1)} custom-call(bf16[16,80,256]{2,1,0:T(8,128)(2,1)} %bitcast.23, f32[2,2,128]{2,1,0:T(2,128)} %gains_ref.1), custom_call_target="tpu_custom_call" | custom-call | tf_op jit(solution)/shard_map/chunk_cotangent/pallas_call | solution.py:261
  18.7 0.6 collective-permute-done
  19.4 1.5 %pad_maximum_fusion = bf16[16,2,8,4608]{3,2,1,0:T(8,128)(2,1)S(1)} fusion(bf16[16,1,8,4608]{3,2,1,0:T(8,128)(2,1)S(1)} %bitcast.22, bf16[16,1,8,4608]{3,2,1,0:T(8,128)(2,1)} %bitcast.21), kind=kLoop, calls=%fused_computation | loop fusion | flops 1179648 | bytes 4718592 | tf_op jit(solution)/shard_map/concatenate | solution.py:265
  20.9 0.0 copy-start
  20.9 0.0 copy-start.1
  20.9 59.2 %conditional.1 = (bf16[16,88,256]{2,1,0:T(8,128)(2,1)S(1)}, bf16[256,4608]{1,0:T(8,128)(2,1)S(1)}) conditional(s32[]{:T(128)} %convert_element_type.3, (bf16[16,88,256]{2,1,0:T(8,128)(2,1)S(1)}, bf16[16,2,8,4608]{3,2,1,0:T(8,128)(2,1)S(1)}) %tuple.20, (bf16[16,2,8,4608]{3,2,1,0:T(8,128)(2,1)S(1)}, bf16[16,88,256]{2,1,0:T(8,128)(2,1)S(1)}) %tuple.21), branch_computations={%region_0.0_spmd, %region_1.0_spmd} | conditional | bytes 6160400 | solution.py:281
  20.9 33.3 %all_to_all.26 = bf16[16,88,256]{2,1,0:T(8,128)(2,1)S(1)} all-to-all(bf16[16,88,256]{2,1,0:T(8,128)(2,1)S(1)} %get-tuple-element.10), channel_id=1, replica_groups=mesh['chip'=16,'core'=2,'seq'=16] {'seq'}, dimensions={0} | all-to-all | bytes 1441792 | tf_op jit(solution)/shard_map/cond/branch_0_fun/all_to_all | solution.py:271
  54.2 25.8 %all_to_all.27 = bf16[16,2,8,4608]{3,2,1,0:T(8,128)(2,1)S(1)} all-to-all(bf16[16,2,8,4608]{3,2,1,0:T(8,128)(2,1)S(1)} %get-tuple-element.12), channel_id=1, replica_groups=mesh['chip'=16,'core'=2,'seq'=16] {'chip'}, dimensions={0} | all-to-all | bytes 4718592 | tf_op jit(solution)/shard_map/cond/branch_0_fun/all_to_all | solution.py:268
  80.0 0.0 copy-start.2
  80.0 0.9 copy-done.2
  80.9 0.0 copy-done
  80.9 0.0 copy-done.1
  80.9 8.5 %attend_pack.1 = (bf16[3,80,4096]{2,1,0:T(8,128)(2,1)}, f32[16,4,128]{2,1,0:T(4,128)S(1)}) custom-call(s32[1]{0:T(128)} %bitcast.2.place_ref, s32[512,32]{1,0:T(8,128)S(1)} %bitcast.17, s32[32,32]{1,0:T(8,128)S(1)} %copy-done.1, bf16[256,4608]{1,0:T(8,128)(2,1)S(1)} %get-tuple-element.27.rows_ref.last_rows_ref, ...), custom_call_target="tpu_custom_call" | custom-call | tf_op jit(solution)/shard_map/attend_pack/pallas_call | solution.py:311
  89.4 15.8 %all_to_all.30 = f32[16,4,128]{2,1,0:T(4,128)S(1)} all-to-all(f32[16,4,128]{2,1,0:T(4,128)S(1)} %get-tuple-element.30), channel_id=1, replica_groups=mesh['chip'=16,'core'=2,'seq'=16] {'seq'}, dimensions={0} | all-to-all | bytes 65536 | tf_op jit(solution)/shard_map/all_to_all | solution.py:312
  105.3 14.6 %all_to_all.31 = f32[32,4,128]{2,1,0:T(4,128)S(1)} all-to-all(f32[32,4,128]{2,1,0:T(4,128)S(1)} %broadcast_in_dim.10), channel_id=1, replica_groups=mesh['chip'=16,'core'=2,'seq'=16] {'chip','core'}, dimensions={0} | all-to-all | bytes 131072 | tf_op jit(solution)/shard_map/all_to_all | solution.py:314
  119.9 0.6 reduce_sum.19
  (2 shorter events, 0.0 us)
Async XLA Ops:
  7.9 11.4 %collective-permute-start = (bf16[128,4608]{1,0:T(8,128)(2,1)}, bf16[128,4608]{1,0:T(8,128)(2,1)S(1)}, u32[]{:S(2)}, u32[]{:S(2)}) collective-permute-start(bf16[128,4608]{1,0:T(8,128)(2,1)} %get-tuple-element.26), channel_id=1, source_target_pairs={{0,16},{16,0},{1,17},{17,1},{2,18},{18,2},{3,19},{19,3},{4,20},{20... | collective-permute-start | bytes 3538952 | tf_op jit(solution)/shard_map/ppermute | solution.py:263
  20.9 60.0 %copy-start = (s32[32,16,32]{2,1,0:T(8,128)S(1)}, s32[32,16,32]{2,1,0:T(8,128)}, u32[]{:S(2)}) copy-start(s32[32,16,32]{2,1,0:T(8,128)} %param.10) | copy-start | bytes 196612
  20.9 60.0 %copy-start.1 = (s32[32,32]{1,0:T(8,128)S(1)}, s32[32,32]{1,0:T(8,128)}, u32[]{:S(2)}) copy-start(s32[32,32]{1,0:T(8,128)} %clip_ref.1) | copy-start | bytes 12292
  80.0 0.9 copy-start.2
where the time goes:
time: 121 us
  blocking collectives  89.6 us (74%)
  Pallas kernels  17.9 us (15%)
  starting transfers between devices  8.74 us (7%)
  other arithmetic  2.14 us (2%)
    all_to_all x1, blocking collectives, move_chunks(): lax.all_to_all(chunks, 'seq', split_axis=0, concat_axis=0, tiled=True)  33.3 us
    all_to_all x1, blocking collectives, move_rows(): return lax.all_to_all(rows, 'chip', split_axis=0, concat_axis=0, tiled=True)  25.8 us
    all_to_all x1, blocking collectives, shards(): lax.all_to_all(gain_parts, 'seq', split_axis=0, concat_axis=0, tiled=True)  15.8 us
    all_to_all x1, blocking collectives, shards(): lax.all_to_all(jnp.broadcast_to(mine, (loaders, 4, head_size)), ('chip',...  14.6 us
    ppermute x1, starting transfers between devices, shards(): other = lax.ppermute(other, 'core', [(0, 1), (1, 0)])  8.74 us
    pallas_call x1, Pallas kernels, shards(): attend(place, table, block_clip, arrived, arrived, chunks)  8.54 us
    pallas_call x1, Pallas kernels, shards(): own, other = gather(place, table, loader_rows.reshape(3 * capacity, width))  7.31 us
  transfers between devices with their start and end apart: 1, of which 1 were waited for; matrix products, arithmetic and copies ran while one was open for 0% of the time, Pallas kernels for 2%

commit v1 on v0

--- a/solution.py
+++ b/solution.py
@@ -29,83 +29,70 @@
 
 
 def gather_kernel(
-    loaders, bands, capacity,
-    place_ref, table_ref, rows_ref, own_ref, other_ref, pick_ref, pick_last_ref, last_ref,
+    flip, loaders, bands, capacity, place_ref, table_ref, rows_ref, out_ref, pick_ref, pick_last_ref, last_ref
 ):
-    step = pl.program_id(0)
-    steps = pl.num_programs(0)
-    lines = loaders * GROUP
-    half = rows_ref.shape[1] // 2
+    peers = loaders // 2
+    lines = peers * GROUP
+    half = 128 * last_ref.shape[0] // 2
+    steps = rows_ref.shape[1] // (2 * half)
     me = place_ref[0]
-
-    @pl.when(step == 0)
-    def _():
-        my_loader = me // bands
-        my_core = my_loader % 2
-        column = iota((1, loaders * bands), 1)
-        band = column % bands
-        target = jnp.where(band == me % bands, column // bands, -1)
-        owner = iota((loaders, 1), 0)
-        owner = 2 * (owner % (loaders // 2)) + (owner // (loaders // 2) + my_core) % 2
-        before = jnp.where((target < owner) & (target >= 0), 1.0, 0.0)
-        same = jnp.where(target == owner, 1.0, 0.0)
-        table = table_ref[...].astype(jnp.float32).astype(jnp.bfloat16)
-        sums = dot(jnp.concatenate([before, same], axis=0).astype(jnp.bfloat16), table)
-        sums = jnp.where(iota(sums.shape, 1) == my_loader, sums, 0.0)
-        sums = jnp.sum(sums, axis=1, keepdims=True)
-        start, count = sums[:loaders].astype(jnp.int32), sums[loaders:].astype(jnp.int32)
-        last_column = jnp.where(count > SLOTS - 1, start + (SLOTS - 1), -1)
-        pick_last_ref[...] = jnp.where(iota((loaders, capacity), 1) == last_column, 1.0, 0.0).astype(jnp.bfloat16)
-        spread = jnp.where(iota((lines, 1), 0) // GROUP == iota((1, loaders), 1), 1.0, 0.0).astype(jnp.bfloat16)
-        wide = dot(spread, jnp.concatenate([start, count], axis=1).astype(jnp.float32).astype(jnp.bfloat16))
-        start, count = wide[:, 0:1].astype(jnp.int32), wide[:, 1:2].astype(jnp.int32)
-        kind = iota((lines, 1), 0) % GROUP
-        slot = kind // 3
-        line_column = jnp.where(slot < count, (kind - 3 * slot) * capacity + start + slot, -1)
-        lanes = iota((lines, 3 * capacity), 1)
-        pick_ref[...] = jnp.where(lanes == line_column, 1.0, 0.0).astype(jnp.bfloat16)
-
-    @pl.when(step < steps - 1)
-    def _():
-        picked = dot(pick_ref[...], rows_ref[...]).astype(jnp.bfloat16)
-        own_ref[...] = picked[: lines // 2]
-        other_ref[...] = picked[lines // 2 :]
-        last = dot(pick_last_ref[...], rows_ref[2 * capacity :])
+    my_loader = me // bands
+    column = iota((1, loaders * bands), 1)
+    target = jnp.where(column % bands == me % bands, column // bands, -1)
+    owner = 2 * iota((peers, 1), 0) + (my_loader + flip) % 2
+    before = jnp.where((target < owner) & (target >= 0), 1.0, 0.0)
+    same = jnp.where(target == owner, 1.0, 0.0)
+    table = table_ref[...].astype(jnp.float32).astype(jnp.bfloat16)
+    sums = dot(jnp.concatenate([before, same], axis=0).astype(jnp.bfloat16), table)
+    sums = jnp.sum(jnp.where(iota(sums.shape, 1) == my_loader, sums, 0.0), axis=1, keepdims=True)
+    start, count = sums[:peers].astype(jnp.int32), sums[peers:].astype(jnp.int32)
+    last_column = jnp.where(count > SLOTS - 1, start + (SLOTS - 1), -1)
+    pick_last_ref[...] = jnp.where(iota((peers, capacity), 1) == last_column, 1.0, 0.0).astype(jnp.bfloat16)
+    spread = jnp.where(iota((lines, 1), 0) // GROUP == iota((1, peers), 1), 1.0, 0.0).astype(jnp.bfloat16)
+    wide = dot(spread, jnp.concatenate([start, count], axis=1).astype(jnp.float32).astype(jnp.bfloat16))
+    start, count = wide[:, 0:1].astype(jnp.int32), wide[:, 1:2].astype(jnp.int32)
+    kind = iota((lines, 1), 0) % GROUP
+    slot = kind // 3
+    line_column = jnp.where(slot < count, (kind - 3 * slot) * capacity + start + slot, -1)
+    lanes = iota((lines, 3 * capacity), 1)
+    pick_ref[...] = jnp.where(lanes == line_column, 1.0, 0.0).astype(jnp.bfloat16)
+    for step in range(steps):
+        at = slice(2 * step * half, 2 * (step + 1) * half)
+        out_ref[:, at] = dot(pick_ref[...], rows_ref[:, at]).astype(jnp.bfloat16)
+        last = dot(pick_last_ref[...], rows_ref[2 * capacity :, at])
         for part in range(2):
-            group = (2 * step + part) % GROUP
+            unit = 2 * step + part
             for low in range(0, half, 128):
-                tile = (2 * step // GROUP) * (half // 128) + low // 128
-                at = part * half + low
-                last_ref[tile, pl.ds(group, loaders, stride=GROUP), :] = last[:, at : at + 128]
-
-    @pl.when(step == steps - 1)
-    def _():
-        for tile in range(last_ref.shape[0]):
-            at = slice(tile * 128, (tile + 1) * 128)
-            last = last_ref[tile].astype(jnp.bfloat16)
-            own_ref[:, at] = last[: lines // 2]
-            other_ref[:, at] = last[lines // 2 :]
+                tile = (unit // GROUP) * (half // 128) + low // 128
+                lane = part * half + low
+                last_ref[tile, pl.ds(unit % GROUP, peers, stride=GROUP), :] = last[:, lane : lane + 128]
+    for tile in range(last_ref.shape[0]):
+        at = slice(rows_ref.shape[1] + tile * 128, rows_ref.shape[1] + (tile + 1) * 128)
+        out_ref[:, at] = last_ref[tile].astype(jnp.bfloat16)
 
 
 def chunk_kernel(capacity, cot_ref, gains_ref, out_ref):
-    gains = gains_ref[...]
-    row = iota((EXTRA, 2 * gains.shape[2]), 0)
+    head_size = out_ref.shape[2]
+    row = iota((EXTRA, head_size), 0)
     extra = jnp.zeros(row.shape, jnp.float32)
     for kind in range(2):
-        line = jnp.concatenate([gains[kind, 0:1], gains[kind, 1:2]], axis=1)
-        for part in range(3):
-            piece = line.astype(jnp.bfloat16).astype(jnp.float32)
-            extra = jnp.where(row == 2 * part + kind, piece, extra)
-            line = line - piece
+        for head in range(2):
+            line = gains_ref[kind, head : head + 1, :]
+            for part in range(2):
+                piece = line.astype(jnp.bfloat16).astype(jnp.float32)
+                extra = jnp.where(row == 4 * part + 2 * kind + head, piece, extra)
+                line = line - piece
     extra = extra.astype(jnp.bfloat16)
     for chunk in range(cot_ref.shape[0]):
-        out_ref[chunk, :capacity] = cot_ref[chunk]
-        out_ref[chunk, capacity:] = extra
+        for head in range(2):
+            lanes = slice(head * head_size, (head + 1) * head_size)
+            out_ref[chunk, head * capacity : (head + 1) * capacity] = cot_ref[chunk, :, lanes]
+        out_ref[chunk, 2 * capacity :] = extra
 
 
 def attention_kernel(
     loaders, bands, capacity, head_size,
-    place_ref, table_ref, clip_ref, rows_ref, last_rows_ref, chunk_ref,
+    place_ref, table_ref, clip_ref, rows_ref, chunk_ref,
     grad_ref, gain_ref,
     pick_ref, pick_last_ref, same_ref,
 ):
@@ -161,19 +148,34 @@
     def average(rows):
         return dot(rows, averager)
 
-    units = chunk_ref.shape[0]
+    units = gain_ref.shape[0]
+    base = units * step
+    features = chunk_ref.shape[0] * width
+    here = pl.ds(pl.multiple_of(base * width, units * width), units * width)
+    last_here = pl.ds(pl.multiple_of(features + base // GROUP * width, width), width)
     pick_last = [
-        jnp.where(group == (units * step + unit) % GROUP, pick_last_ref[...], jnp.zeros((), bfloat))
+        jnp.where(group == (base + unit) % GROUP, pick_last_ref[...], jnp.zeros((), bfloat))
         for unit in range(units)
     ]
-    packed = dot(pick_ref[...], rows_ref[...])
-    last = dot(jnp.concatenate(pick_last, axis=0), last_rows_ref[...])
+    packed = dot(pick_ref[...], rows_ref[:, here])
+    last = dot(jnp.concatenate(pick_last, axis=0), rows_ref[:, last_here])
     lane = [slice(unit * width, (unit + 1) * width) for unit in range(units)]
     span = [slice(unit * capacity, (unit + 1) * capacity) for unit in range(units)]
     value = [(packed[2 * capacity :, lane[u]] + last[span[u]]).astype(bfloat) for u in range(units)]
-    extra = [chunk_ref[u, capacity:].astype(jnp.float32) for u in range(units)]
-    gains = [rows[0:2] + rows[2:4] + rows[4:6] for rows in extra]
-    dout = [jnp.where(valid, chunk_ref[u, :capacity], jnp.zeros((), bfloat)) for u in range(units)]
+    extra = [chunk_ref[base + u, 2 * capacity :].astype(jnp.float32) for u in range(units)]
+    extra = [rows[0:4] + rows[4:8] for rows in extra]
+    gains = [
+        jnp.concatenate(
+            [jnp.concatenate([rows[2 * kind : 2 * kind + 1], rows[2 * kind + 1 : 2 * kind + 2]], axis=1) for kind in range(2)],
+            axis=0,
+        )
+        for rows in extra
+    ]
+    dout = [
+        jnp.where(valid, chunk_ref[base + u, head * capacity : (head + 1) * capacity], jnp.zeros((), bfloat))
+        for u in range(units)
+        for head in range(2)
+    ]
     raw = jnp.concatenate(
         [packed[part * capacity : (part + 1) * capacity, lane[u]] for part in range(2) for u in range(units)], axis=0
     )
@@ -185,7 +187,7 @@
     kn = [(hats[1][u] * gains[u][1:2]).astype(bfloat) for u in range(units)]
     each = [(u, lanes) for u in range(units) for lanes in heads]
     score = [dot(kn[u][:, lanes], qn[u][:, lanes], 1, 1) for u, lanes in each]
-    dprob = [dot(value[u][:, lanes], dout[u][:, lanes], 1, 1) for u, lanes in each]
+    dprob = [dot(value[u][:, lanes], dout[n], 1, 1) for n, (u, lanes) in enumerate(each)]
     weight = [jnp.where(same, jnp.exp(rows * scale), 0.0) for rows in score]
     prob = [rows * (1.0 / jnp.sum(rows, axis=0, keepdims=True)) for rows in weight]
     delta = [jnp.sum(p * d, axis=0, keepdims=True) for p, d in zip(prob, dprob)]
@@ -194,7 +196,7 @@
         [dot(dscore[n], kn[u][:, lanes], 0, 0) for n, (u, lanes) in enumerate(each)],
         [dot(dscore[n], qn[u][:, lanes]) for n, (u, lanes) in enumerate(each)],
     ]
-    dvalue = [dot(prob[n].astype(bfloat), dout[u][:, lanes]) for n, (u, lanes) in enumerate(each)]
+    dvalue = [dot(prob[n].astype(bfloat), dout[n]) for n in range(len(each))]
     for n, (u, lanes) in enumerate(each):
         grad_ref[2, :, u * width + lanes.start : u * width + lanes.stop] = dvalue[n].astype(bfloat)
     scaled, seconds = [], []
@@ -229,38 +231,37 @@
     place = lax.axis_index(("chip", "core", "seq")).astype(jnp.int32).reshape(1)
     table = block_rows.reshape(loaders * bands, loaders)
     smem = pl.BlockSpec(memory_space=pltpu.SMEM)
-
-    gather = pl.pallas_call(
-        functools.partial(gather_kernel, loaders, bands, capacity),
-        grid=(width // (2 * pair) + 1,),
-        in_specs=[
-            smem,
-            pl.BlockSpec((loaders * bands, loaders), lambda t: (0, 0)),
-            pl.BlockSpec((3 * capacity, 2 * pair), lambda t: (0, jnp.minimum(t, width // (2 * pair) - 1))),
-        ],
-        out_specs=[pl.BlockSpec((lines // 2, 2 * pair), lambda t: (0, t))] * 2,
-        out_shape=[jax.ShapeDtypeStruct((lines // 2, width + 2 * pair), jnp.bfloat16)] * 2,
-        scratch_shapes=[
-            pltpu.VMEM((lines, 3 * capacity), jnp.bfloat16),
-            pltpu.VMEM((loaders, capacity), jnp.bfloat16),
-            pltpu.VMEM((2 * pair // 128, lines, 128), jnp.float32),
-        ],
-        name="gather_rows",
-    )
+    vmem = pl.BlockSpec(memory_space=pltpu.VMEM)
+
+    vmem = pl.BlockSpec(memory_space=pltpu.VMEM)
+    def gather(flip):
+        return pl.pallas_call(
+            functools.partial(gather_kernel, flip, loaders, bands, capacity),
+            in_specs=[smem, vmem, vmem],
+            out_specs=vmem,
+            out_shape=jax.ShapeDtypeStruct((lines // 2, width + 2 * pair), jnp.bfloat16),
+            scratch_shapes=[
+                pltpu.VMEM((lines // 2, 3 * capacity), jnp.bfloat16),
+                pltpu.VMEM((loaders // 2, capacity), jnp.bfloat16),
+                pltpu.VMEM((2 * pair // 128, lines // 2, 128), jnp.float32),
+            ],
+            compiler_params=pltpu.CompilerParams(vmem_limit_bytes=8 << 20),
+            cost_estimate=pl.CostEstimate(flops=300_000_000, bytes_accessed=3_000_000, transcendentals=0),
+            name="gather_rows" if flip else "gather_own",
+        )(place, table, loader_rows.reshape(3 * capacity, width))
+
     pack = pl.pallas_call(
         functools.partial(chunk_kernel, capacity),
-        grid=(4,),
-        in_specs=[
-            pl.BlockSpec((bands // 4, capacity, pair), lambda t: (t, 0, 0)),
-            pl.BlockSpec((2, 2, head_size), lambda t: (0, 0, 0)),
-        ],
-        out_specs=pl.BlockSpec((bands // 4, capacity + EXTRA, pair), lambda t: (t, 0, 0)),
-        out_shape=jax.ShapeDtypeStruct((bands, capacity + EXTRA, pair), jnp.bfloat16),
+        in_specs=[vmem, vmem],
+        out_specs=vmem,
+        out_shape=jax.ShapeDtypeStruct((bands, 2 * capacity + EXTRA, head_size), jnp.bfloat16),
+        compiler_params=pltpu.CompilerParams(vmem_limit_bytes=8 << 20),
         name="chunk_cotangent",
     )
     chunks = pack(cotangent.reshape(bands, capacity, pair), gains)
-    own, other = gather(place, table, loader_rows.reshape(3 * capacity, width))
+    other = gather(1)
     other = lax.ppermute(other, "core", [(0, 1), (1, 0)])
+    own = gather(0)
     shape = (loaders // 2, 1, GROUP, width + 2 * pair)
     outgoing = jnp.concatenate([own.reshape(shape), other.reshape(shape)], axis=1)
 
@@ -288,9 +289,8 @@
             smem,
             pl.BlockSpec((loaders * bands, loaders), lambda t: (0, 0)),
             pl.BlockSpec((loaders, loaders), lambda t: (0, 0)),
-            pl.BlockSpec((lines, 4 * pair), lambda t: (0, t)),
-            pl.BlockSpec((lines, pair), lambda t: (0, pairs + 4 * t // GROUP)),
-            pl.BlockSpec((4, capacity + EXTRA, pair), lambda t: (t, 0, 0)),
+            vmem,
+            vmem,
         ],
         out_specs=[
             pl.BlockSpec((3, capacity, 4 * pair), lambda t: (0, 0, t)),
@@ -308,7 +308,7 @@
         compiler_params=pltpu.CompilerParams(vmem_limit_bytes=16 << 20),
         name="attend_pack",
     )
-    gradients, gain_parts = attend(place, table, block_clip, arrived, arrived, chunks)
+    gradients, gain_parts = attend(place, table, block_clip, arrived, chunks)
     by_head = lax.all_to_all(gain_parts, "seq", split_axis=0, concat_axis=0, tiled=True)
     mine = jnp.sum(by_head, axis=0, keepdims=True)
     every = lax.all_to_all(

time: 121 us -> 114 us (0.942)
  Pallas kernels: 17.9 us -> 9.96 us
  local copies, waits for them, and re-layouts: 0.88 us -> 3.6 us
    pallas_call x2 -> x3, Pallas kernels: 15.8 us -> 9.84 us  [the longest x1 7.32 us: shards(): gradients, gain_parts = attend(place, table, block_clip, arrived, chunks)]
    unnamed x6 -> x14, local copies, waits for them, and re-layouts: 0.87 us -> 3.59 us
    pallas_call x1, Pallas kernels: 2.02 us -> 0.12 us  [shards(): chunks = pack(cotangent.reshape(bands, capacity, pair), gains)]
  transfers between devices with their start and end apart: 1 -> 1, of which waited for: 1 -> 1; matrix products, arithmetic and copies ran while one was open for 0% -> 0% of each run, Pallas kernels for 2% -> 1%
where the time goes in v1:
time: 114 us
  blocking collectives  88.7 us (78%)
  Pallas kernels  9.96 us (9%)
  starting transfers between devices  8.75 us (8%)
  local copies, waits for them, and re-layouts  3.6 us (3%)
  other arithmetic  2.14 us (2%)
    all_to_all x1, blocking collectives, move_chunks(): lax.all_to_all(chunks, 'seq', split_axis=0, concat_axis=0, tiled=True)  32.8 us
    all_to_all x1, blocking collectives, move_rows(): return lax.all_to_all(rows, 'chip', split_axis=0, concat_axis=0, tiled=True)  25.8 us
    all_to_all x1, blocking collectives, shards(): lax.all_to_all(gain_parts, 'seq', split_axis=0, concat_axis=0, tiled=True)  15.6 us
    all_to_all x1, blocking collectives, shards(): lax.all_to_all(jnp.broadcast_to(mine, (loaders, 4, head_size)), ('chip',...  14.6 us
    ppermute x1, starting transfers between devices, shards(): other = lax.ppermute(other, 'core', [(0, 1), (1, 0)])  8.75 us
    pallas_call x1, Pallas kernels, shards(): gradients, gain_parts = attend(place, table, block_clip, arrived, chunks)  7.32 us
    unnamed x14, local copies, waits for them, and re-layouts  3.59 us
    pallas_call x2, Pallas kernels, gather(): pl.pallas_call(functools.partial(gather_kernel, flip, loaders, bands, cap...  2.52 us
  transfers between devices with their start and end apart: 1, of which 1 were waited for; matrix products, arithmetic and copies ran while one was open for 0% of the time, Pallas kernels for 1%

profile of v1, /device:TPU:1, one launch (start us, length us, event | category | flops | bytes accessed | tf_op | source)
XLA Modules:
  0.0 114.0 jit_solution(4867410166658044530)
XLA Ops:
  0.6 0.0 copy-start.6
  0.6 0.0 copy-start
  0.7 1.5 %copy-done = bf16[3,1,80,4096]{3,2,1,0:T(8,128)(2,1)S(1)} copy-done((bf16[3,1,80,4096]{3,2,1,0:T(8,128)(2,1)S(1)}, bf16[3,1,80,4096]{3,2,1,0:T(8,128)(2,1)}, u32[]{:S(2)}) %copy-start) | copy-done | bytes 1966104
  2.2 0.0 copy-start.2
  2.2 0.9 copy-done.2
  3.1 0.0 copy-start.1
  3.1 0.0 copy-start.3
  3.2 1.3 %gather_rows.1 = bf16[128,4608]{1,0:T(8,128)(2,1)S(1)} custom-call(s32[1]{0:T(128)} %bitcast.2.place_ref, s32[512,32]{1,0:T(8,128)S(1)} %bitcast.19, bf16[240,4096]{1,0:T(8,128)(2,1)S(1)} %bitcast.16), custom_call_target="tpu_custom_call" | custom-call | flops 300000000 | bytes 3000000 | tf_op jit(solution)/shard_map/gather_rows/pallas_call | solution.py:238
  4.4 8.7 %collective-permute-start = (bf16[128,4608]{1,0:T(8,128)(2,1)S(1)}, bf16[128,4608]{1,0:T(8,128)(2,1)}, u32[]{:S(2)}, u32[]{:S(2)}) collective-permute-start(bf16[128,4608]{1,0:T(8,128)(2,1)S(1)} %gather_rows.1), channel_id=1, source_target_pairs={{0,16},{16,0},{1,17},{17,1},{2,18},{18,2},{3,19},{19,3},{4,20},{20... | collective-permute-start | bytes 3538952 | tf_op jit(solution)/shard_map/ppermute | solution.py:263
  13.2 0.0 copy-done.6
  13.2 0.0 copy-start.4
  13.2 1.1 copy-done.4
  14.3 0.1 chunk_cotangent.1
  14.4 0.0 copy-done.1
  14.4 0.0 copy-done.3
  14.4 1.3 %gather_own.1 = bf16[128,4608]{1,0:T(8,128)(2,1)S(1)} custom-call(s32[1]{0:T(128)} %bitcast.2.place_ref, s32[512,32]{1,0:T(8,128)S(1)} %bitcast.20, bf16[240,4096]{1,0:T(8,128)(2,1)S(1)} %bitcast.17), custom_call_target="tpu_custom_call" | custom-call | flops 300000000 | bytes 3000000 | tf_op jit(solution)/shard_map/gather_own/pallas_call | solution.py:238
  15.7 0.1 collective-permute-done
  15.8 1.5 %pad_maximum_fusion = bf16[16,2,8,4608]{3,2,1,0:T(8,128)(2,1)S(1)} fusion(bf16[16,1,8,4608]{3,2,1,0:T(8,128)(2,1)} %bitcast.9, bf16[16,1,8,4608]{3,2,1,0:T(8,128)(2,1)S(1)} %bitcast.18), kind=kLoop, calls=%fused_computation | loop fusion | flops 1179648 | bytes 4718592 | tf_op jit(solution)/shard_map/concatenate | solution.py:266
  17.3 0.0 copy-start.5
  17.3 58.6 %conditional.1 = (bf16[16,168,128]{2,1,0:T(8,128)(2,1)S(1)}, bf16[256,4608]{1,0:T(8,128)(2,1)S(1)}) conditional(s32[]{:T(128)} %convert_element_type.3, (bf16[16,168,128]{2,1,0:T(8,128)(2,1)S(1)}, bf16[16,2,8,4608]{3,2,1,0:T(8,128)(2,1)S(1)}) %tuple.20, (bf16[16,2,8,4608]{3,2,1,0:T(8,128)(2,1)S(1)}, bf16[16,168,128]{2,1,0:T(8,128)(2,1)S(1)}) %tuple.21), branch_computations={%region_0.0_spmd, %region_1.0_spmd} | conditional | bytes 6094864 | solution.py:282
  17.3 32.8 %all_to_all.26 = bf16[16,168,128]{2,1,0:T(8,128)(2,1)S(1)} all-to-all(bf16[16,168,128]{2,1,0:T(8,128)(2,1)S(1)} %get-tuple-element.10), channel_id=1, replica_groups=mesh['chip'=16,'core'=2,'seq'=16] {'seq'}, dimensions={0} | all-to-all | bytes 1376256 | tf_op jit(solution)/shard_map/cond/branch_0_fun/all_to_all | solution.py:272
  50.0 25.8 %all_to_all.27 = bf16[16,2,8,4608]{3,2,1,0:T(8,128)(2,1)S(1)} all-to-all(bf16[16,2,8,4608]{3,2,1,0:T(8,128)(2,1)S(1)} %get-tuple-element.12), channel_id=1, replica_groups=mesh['chip'=16,'core'=2,'seq'=16] {'chip'}, dimensions={0} | all-to-all | bytes 4718592 | tf_op jit(solution)/shard_map/cond/branch_0_fun/all_to_all | solution.py:269
  75.8 0.0 copy-done.5
  75.8 7.3 %attend_pack.1 = (bf16[3,80,4096]{2,1,0:T(8,128)(2,1)}, f32[16,4,128]{2,1,0:T(4,128)S(1)}) custom-call(s32[1]{0:T(128)} %bitcast.2.place_ref, s32[512,32]{1,0:T(8,128)S(1)} %bitcast.21, s32[32,32]{1,0:T(8,128)S(1)} %copy-done.5, bf16[256,4608]{1,0:T(8,128)(2,1)S(1)} %get-tuple-element.23.rows_ref, bf16[16,168,128]{2,1,0:T(8,128)(2,1)S(1)} %get-tuple-element.24.chunk_ref), custom_call_target="tpu_custom_call" | custom-call | tf_op jit(solution)/shard_map/attend_pack/pallas_call | solution.py:311
  83.1 15.6 %all_to_all.30 = f32[16,4,128]{2,1,0:T(4,128)S(1)} all-to-all(f32[16,4,128]{2,1,0:T(4,128)S(1)} %get-tuple-element.26), channel_id=1, replica_groups=mesh['chip'=16,'core'=2,'seq'=16] {'seq'}, dimensions={0} | all-to-all | bytes 65536 | tf_op jit(solution)/shard_map/all_to_all | solution.py:312
  98.7 14.6 %all_to_all.31 = f32[32,4,128]{2,1,0:T(4,128)S(1)} all-to-all(f32[32,4,128]{2,1,0:T(4,128)S(1)} %broadcast_in_dim.10), channel_id=1, replica_groups=mesh['chip'=16,'core'=2,'seq'=16] {'chip','core'}, dimensions={0} | all-to-all | bytes 131072 | tf_op jit(solution)/shard_map/all_to_all | solution.py:314
  113.4 0.6 reduce_sum.19
  (2 shorter events, 0.0 us)
Async XLA Ops:
  0.6 12.6 %copy-start.6 = (f32[2,2,128]{2,1,0:T(2,128)S(1)}, f32[2,2,128]{2,1,0:T(2,128)}, u32[]{:S(2)}) copy-start(f32[2,2,128]{2,1,0:T(2,128)} %gains_ref.1) | copy-start | bytes 6148
  0.6 1.5 %copy-start = (bf16[3,1,80,4096]{3,2,1,0:T(8,128)(2,1)S(1)}, bf16[3,1,80,4096]{3,2,1,0:T(8,128)(2,1)}, u32[]{:S(2)}) copy-start(bf16[3,1,80,4096]{3,2,1,0:T(8,128)(2,1)} %param.7) | copy-start | bytes 5898244
  2.2 0.9 copy-start.2
  3.1 11.3 %copy-start.1 = (bf16[3,1,80,4096]{3,2,1,0:T(8,128)(2,1)S(1)}, bf16[3,1,80,4096]{3,2,1,0:T(8,128)(2,1)}, u32[]{:S(2)}) copy-start(bf16[3,1,80,4096]{3,2,1,0:T(8,128)(2,1)} %param.7) | copy-start | bytes 5898244
  3.1 11.3 %copy-start.3 = (s32[32,16,32]{2,1,0:T(8,128)S(1)}, s32[32,16,32]{2,1,0:T(8,128)}, u32[]{:S(2)}) copy-start(s32[32,16,32]{2,1,0:T(8,128)} %param.10) | copy-start | bytes 196612
  4.4 11.3 %collective-permute-start = (bf16[128,4608]{1,0:T(8,128)(2,1)S(1)}, bf16[128,4608]{1,0:T(8,128)(2,1)}, u32[]{:S(2)}, u32[]{:S(2)}) collective-permute-start(bf16[128,4608]{1,0:T(8,128)(2,1)S(1)} %gather_rows.1), channel_id=1, source_target_pairs={{0,16},{16,0},{1,17},{17,1},{2,18},{18,2},{3,19},{19,3},{4,20},{20... | collective-permute-start | bytes 3538952 | tf_op jit(solution)/shard_map/ppermute | solution.py:263
  13.2 1.1 copy-start.4
  17.3 58.6 %copy-start.5 = (s32[32,32]{1,0:T(8,128)S(1)}, s32[32,32]{1,0:T(8,128)}, u32[]{:S(2)}) copy-start(s32[32,32]{1,0:T(8,128)} %clip_ref.1) | copy-start | bytes 12292

commit v2 on v1

--- a/solution.py
+++ b/solution.py
@@ -148,6 +148,10 @@
     def average(rows):
         return dot(rows, averager)
 
+    def lane_average(rows):
+        means = [jnp.mean(rows[:, lanes], axis=1, keepdims=True) for lanes in heads]
+        return jnp.concatenate([jnp.broadcast_to(m, (rows.shape[0], head_size)) for m in means], axis=1)
+
     units = gain_ref.shape[0]
     base = units * step
     features = chunk_ref.shape[0] * width
@@ -180,7 +184,7 @@
         [packed[part * capacity : (part + 1) * capacity, lane[u]] for part in range(2) for u in range(units)], axis=0
     )
     centred = raw - average(raw.astype(bfloat))
-    factor = lax.rsqrt(average((centred * centred).astype(bfloat)) + epsilon)
+    factor = lax.rsqrt(lane_average(centred * centred) + epsilon)
     hat = centred * factor
     hats = [[hat[(part * units + u) * capacity :][:capacity] for u in range(units)] for part in range(2)]
     qn = [(hats[0][u] * gains[u][0:1]).astype(bfloat) for u in range(units)]
@@ -211,7 +215,7 @@
             scaled.append(grad * gain)
             seconds.append(product * gain)
     scaled = jnp.concatenate(scaled, axis=0)
-    first = average(scaled.astype(bfloat))
+    first = lane_average(scaled)
     second = average(jnp.concatenate(seconds, axis=0).astype(bfloat))
     result = (factor * (scaled - first - hat * second)).astype(bfloat)
     for part in range(2):
@@ -284,7 +288,7 @@
 
     attend = pl.pallas_call(
         functools.partial(attention_kernel, loaders, bands, capacity, head_size),
-        grid=(pairs // 4,),
+        grid=(pairs // 8,),
         in_specs=[
             smem,
             pl.BlockSpec((loaders * bands, loaders), lambda t: (0, 0)),
@@ -293,8 +297,8 @@
             vmem,
         ],
         out_specs=[
-            pl.BlockSpec((3, capacity, 4 * pair), lambda t: (0, 0, t)),
-            pl.BlockSpec((4, 4, head_size), lambda t: (t, 0, 0)),
+            pl.BlockSpec((3, capacity, 8 * pair), lambda t: (0, 0, t)),
+            pl.BlockSpec((8, 4, head_size), lambda t: (t, 0, 0)),
         ],
         out_shape=[
             jax.ShapeDtypeStruct((3, capacity, width), jnp.bfloat16),
@@ -305,7 +309,7 @@
             pltpu.VMEM((capacity, lines), jnp.bfloat16),
             pltpu.VMEM((capacity, capacity), jnp.float32),
         ],
-        compiler_params=pltpu.CompilerParams(vmem_limit_bytes=16 << 20),
+        compiler_params=pltpu.CompilerParams(vmem_limit_bytes=24 << 20),
         name="attend_pack",
     )
     gradients, gain_parts = attend(place, table, block_clip, arrived, chunks)

time: 114 us -> 113 us (level)
  Pallas kernels: 9.96 us -> 8.61 us
    pallas_call x1, Pallas kernels: 7.32 us -> 5.97 us  [shards(): gradients, gain_parts = attend(place, table, block_clip, arrived, chunks)]
where the time goes in v2:
time: 113 us
  blocking collectives  88.7 us (78%)
  starting transfers between devices  8.75 us (8%)
  Pallas kernels  8.61 us (8%)
  local copies, waits for them, and re-layouts  3.6 us (3%)
  other arithmetic  2.14 us (2%)
    all_to_all x1, blocking collectives, move_chunks(): lax.all_to_all(chunks, 'seq', split_axis=0, concat_axis=0, tiled=True)  32.8 us
    all_to_all x1, blocking collectives, move_rows(): return lax.all_to_all(rows, 'chip', split_axis=0, concat_axis=0, tiled=True)  25.8 us
    all_to_all x1, blocking collectives, shards(): lax.all_to_all(gain_parts, 'seq', split_axis=0, concat_axis=0, tiled=True)  15.6 us
    all_to_all x1, blocking collectives, shards(): lax.all_to_all(jnp.broadcast_to(mine, (loaders, 4, head_size)), ('chip',...  14.6 us
    ppermute x1, starting transfers between devices, shards(): other = lax.ppermute(other, 'core', [(0, 1), (1, 0)])  8.75 us
    pallas_call x1, Pallas kernels, shards(): gradients, gain_parts = attend(place, table, block_clip, arrived, chunks)  5.97 us
    unnamed x14, local copies, waits for them, and re-layouts  3.59 us
    pallas_call x2, Pallas kernels, gather(): pl.pallas_call(functools.partial(gather_kernel, flip, loaders, bands, cap...  2.52 us
  transfers between devices with their start and end apart: 1, of which 1 were waited for; matrix products, arithmetic and copies ran while one was open for 0% of the time, Pallas kernels for 1%

profile of v2, /device:TPU:1, one launch (start us, length us, event | category | flops | bytes accessed | tf_op | source)
XLA Modules:
  0.0 112.6 jit_solution(2020042526321541319)
XLA Ops:
  0.6 0.0 copy-start.6
  0.6 0.0 copy-start
  0.7 1.5 %copy-done = bf16[3,1,80,4096]{3,2,1,0:T(8,128)(2,1)S(1)} copy-done((bf16[3,1,80,4096]{3,2,1,0:T(8,128)(2,1)S(1)}, bf16[3,1,80,4096]{3,2,1,0:T(8,128)(2,1)}, u32[]{:S(2)}) %copy-start) | copy-done | bytes 1966104
  2.2 0.0 copy-start.2
  2.2 0.9 copy-done.2
  3.1 0.0 copy-start.1
  3.1 0.0 copy-start.3
  3.2 1.3 %gather_rows.1 = bf16[128,4608]{1,0:T(8,128)(2,1)S(1)} custom-call(s32[1]{0:T(128)} %bitcast.2.place_ref, s32[512,32]{1,0:T(8,128)S(1)} %bitcast.19, bf16[240,4096]{1,0:T(8,128)(2,1)S(1)} %bitcast.16), custom_call_target="tpu_custom_call" | custom-call | flops 300000000 | bytes 3000000 | tf_op jit(solution)/shard_map/gather_rows/pallas_call | solution.py:242
  4.4 8.7 %collective-permute-start = (bf16[128,4608]{1,0:T(8,128)(2,1)S(1)}, bf16[128,4608]{1,0:T(8,128)(2,1)}, u32[]{:S(2)}, u32[]{:S(2)}) collective-permute-start(bf16[128,4608]{1,0:T(8,128)(2,1)S(1)} %gather_rows.1), channel_id=1, source_target_pairs={{0,16},{16,0},{1,17},{17,1},{2,18},{18,2},{3,19},{19,3},{4,20},{20... | collective-permute-start | bytes 3538952 | tf_op jit(solution)/shard_map/ppermute | solution.py:267
  13.2 0.0 copy-done.6
  13.2 0.0 copy-start.4
  13.2 1.1 copy-done.4
  14.3 0.1 chunk_cotangent.1
  14.4 0.0 copy-done.1
  14.4 0.0 copy-done.3
  14.4 1.3 %gather_own.1 = bf16[128,4608]{1,0:T(8,128)(2,1)S(1)} custom-call(s32[1]{0:T(128)} %bitcast.2.place_ref, s32[512,32]{1,0:T(8,128)S(1)} %bitcast.20, bf16[240,4096]{1,0:T(8,128)(2,1)S(1)} %bitcast.17), custom_call_target="tpu_custom_call" | custom-call | flops 300000000 | bytes 3000000 | tf_op jit(solution)/shard_map/gather_own/pallas_call | solution.py:242
  15.7 0.1 collective-permute-done
  15.8 1.5 %pad_maximum_fusion = bf16[16,2,8,4608]{3,2,1,0:T(8,128)(2,1)S(1)} fusion(bf16[16,1,8,4608]{3,2,1,0:T(8,128)(2,1)} %bitcast.9, bf16[16,1,8,4608]{3,2,1,0:T(8,128)(2,1)S(1)} %bitcast.18), kind=kLoop, calls=%fused_computation | loop fusion | flops 1179648 | bytes 4718592 | tf_op jit(solution)/shard_map/concatenate | solution.py:270
  17.3 0.0 copy-start.5
  17.3 58.6 %conditional.1 = (bf16[16,168,128]{2,1,0:T(8,128)(2,1)S(1)}, bf16[256,4608]{1,0:T(8,128)(2,1)S(1)}) conditional(s32[]{:T(128)} %convert_element_type.3, (bf16[16,168,128]{2,1,0:T(8,128)(2,1)S(1)}, bf16[16,2,8,4608]{3,2,1,0:T(8,128)(2,1)S(1)}) %tuple.20, (bf16[16,2,8,4608]{3,2,1,0:T(8,128)(2,1)S(1)}, bf16[16,168,128]{2,1,0:T(8,128)(2,1)S(1)}) %tuple.21), branch_computations={%region_0.0_spmd, %region_1.0_spmd} | conditional | bytes 6094864 | solution.py:286
  17.3 32.8 %all_to_all.26 = bf16[16,168,128]{2,1,0:T(8,128)(2,1)S(1)} all-to-all(bf16[16,168,128]{2,1,0:T(8,128)(2,1)S(1)} %get-tuple-element.10), channel_id=1, replica_groups=mesh['chip'=16,'core'=2,'seq'=16] {'seq'}, dimensions={0} | all-to-all | bytes 1376256 | tf_op jit(solution)/shard_map/cond/branch_0_fun/all_to_all | solution.py:276
  50.0 25.8 %all_to_all.27 = bf16[16,2,8,4608]{3,2,1,0:T(8,128)(2,1)S(1)} all-to-all(bf16[16,2,8,4608]{3,2,1,0:T(8,128)(2,1)S(1)} %get-tuple-element.12), channel_id=1, replica_groups=mesh['chip'=16,'core'=2,'seq'=16] {'chip'}, dimensions={0} | all-to-all | bytes 4718592 | tf_op jit(solution)/shard_map/cond/branch_0_fun/all_to_all | solution.py:273
  75.8 0.0 copy-done.5
  75.8 6.0 %attend_pack.1 = (bf16[3,80,4096]{2,1,0:T(8,128)(2,1)}, f32[16,4,128]{2,1,0:T(4,128)S(1)}) custom-call(s32[1]{0:T(128)} %bitcast.2.place_ref, s32[512,32]{1,0:T(8,128)S(1)} %bitcast.21, s32[32,32]{1,0:T(8,128)S(1)} %copy-done.5, bf16[256,4608]{1,0:T(8,128)(2,1)S(1)} %get-tuple-element.23.rows_ref, bf16[16,168,128]{2,1,0:T(8,128)(2,1)S(1)} %get-tuple-element.24.chunk_ref), custom_call_target="tpu_custom_call" | custom-call | tf_op jit(solution)/shard_map/attend_pack/pallas_call | solution.py:315
  81.8 15.6 %all_to_all.30 = f32[16,4,128]{2,1,0:T(4,128)S(1)} all-to-all(f32[16,4,128]{2,1,0:T(4,128)S(1)} %get-tuple-element.26), channel_id=1, replica_groups=mesh['chip'=16,'core'=2,'seq'=16] {'seq'}, dimensions={0} | all-to-all | bytes 65536 | tf_op jit(solution)/shard_map/all_to_all | solution.py:316
  97.4 14.6 %all_to_all.31 = f32[32,4,128]{2,1,0:T(4,128)S(1)} all-to-all(f32[32,4,128]{2,1,0:T(4,128)S(1)} %broadcast_in_dim.10), channel_id=1, replica_groups=mesh['chip'=16,'core'=2,'seq'=16] {'chip','core'}, dimensions={0} | all-to-all | bytes 131072 | tf_op jit(solution)/shard_map/all_to_all | solution.py:318
  112.0 0.6 reduce_sum.19
  (2 shorter events, 0.0 us)
Async XLA Ops:
  0.6 12.6 %copy-start.6 = (f32[2,2,128]{2,1,0:T(2,128)S(1)}, f32[2,2,128]{2,1,0:T(2,128)}, u32[]{:S(2)}) copy-start(f32[2,2,128]{2,1,0:T(2,128)} %gains_ref.1) | copy-start | bytes 6148
  0.6 1.5 %copy-start = (bf16[3,1,80,4096]{3,2,1,0:T(8,128)(2,1)S(1)}, bf16[3,1,80,4096]{3,2,1,0:T(8,128)(2,1)}, u32[]{:S(2)}) copy-start(bf16[3,1,80,4096]{3,2,1,0:T(8,128)(2,1)} %param.7) | copy-start | bytes 5898244
  2.2 0.9 copy-start.2
  3.1 11.3 %copy-start.1 = (bf16[3,1,80,4096]{3,2,1,0:T(8,128)(2,1)S(1)}, bf16[3,1,80,4096]{3,2,1,0:T(8,128)(2,1)}, u32[]{:S(2)}) copy-start(bf16[3,1,80,4096]{3,2,1,0:T(8,128)(2,1)} %param.7) | copy-start | bytes 5898244
  3.1 11.3 %copy-start.3 = (s32[32,16,32]{2,1,0:T(8,128)S(1)}, s32[32,16,32]{2,1,0:T(8,128)}, u32[]{:S(2)}) copy-start(s32[32,16,32]{2,1,0:T(8,128)} %param.10) | copy-start | bytes 196612
  4.4 11.3 %collective-permute-start = (bf16[128,4608]{1,0:T(8,128)(2,1)S(1)}, bf16[128,4608]{1,0:T(8,128)(2,1)}, u32[]{:S(2)}, u32[]{:S(2)}) collective-permute-start(bf16[128,4608]{1,0:T(8,128)(2,1)S(1)} %gather_rows.1), channel_id=1, source_target_pairs={{0,16},{16,0},{1,17},{17,1},{2,18},{18,2},{3,19},{19,3},{4,20},{20... | collective-permute-start | bytes 3538952 | tf_op jit(solution)/shard_map/ppermute | solution.py:267
  13.2 1.1 copy-start.4
  17.3 58.6 %copy-start.5 = (s32[32,32]{1,0:T(8,128)S(1)}, s32[32,32]{1,0:T(8,128)}, u32[]{:S(2)}) copy-start(s32[32,32]{1,0:T(8,128)} %clip_ref.1) | copy-start | bytes 12292

commit v3 on v2

--- a/solution.py
+++ b/solution.py
@@ -152,7 +152,7 @@
         means = [jnp.mean(rows[:, lanes], axis=1, keepdims=True) for lanes in heads]
         return jnp.concatenate([jnp.broadcast_to(m, (rows.shape[0], head_size)) for m in means], axis=1)
 
-    units = gain_ref.shape[0]
+    units = gain_ref.shape[1]
     base = units * step
     features = chunk_ref.shape[0] * width
     here = pl.ds(pl.multiple_of(base * width, units * width), units * width)
@@ -211,7 +211,8 @@
             product = grad * hats[part][u]
             total_gain = jnp.sum(product, axis=0, keepdims=True) * scale
             for head, lanes in enumerate(heads):
-                gain_ref[u, 2 * part + head : 2 * part + head + 1, :] = total_gain[:, lanes]
+                for copy in range(2):
+                    gain_ref[copy, u, 2 * part + head : 2 * part + head + 1, :] = total_gain[:, lanes]
             scaled.append(grad * gain)
             seconds.append(product * gain)
     scaled = jnp.concatenate(scaled, axis=0)
@@ -298,11 +299,11 @@
         ],
         out_specs=[
             pl.BlockSpec((3, capacity, 8 * pair), lambda t: (0, 0, t)),
-            pl.BlockSpec((8, 4, head_size), lambda t: (t, 0, 0)),
+            pl.BlockSpec((2, 8, 4, head_size), lambda t: (0, t, 0, 0)),
         ],
         out_shape=[
             jax.ShapeDtypeStruct((3, capacity, width), jnp.bfloat16),
-            jax.ShapeDtypeStruct((bands, 4, head_size), jnp.float32),
+            jax.ShapeDtypeStruct((2, bands, 4, head_size), jnp.float32),
         ],
         scratch_shapes=[
             pltpu.VMEM((3 * capacity, lines), jnp.bfloat16),
@@ -313,10 +314,12 @@
         name="attend_pack",
     )
     gradients, gain_parts = attend(place, table, block_clip, arrived, chunks)
-    by_head = lax.all_to_all(gain_parts, "seq", split_axis=0, concat_axis=0, tiled=True)
+    by_head = lax.all_to_all(
+        gain_parts.reshape(2 * bands, 4, head_size), ("core", "seq"), split_axis=0, concat_axis=0, tiled=True
+    )
     mine = jnp.sum(by_head, axis=0, keepdims=True)
     every = lax.all_to_all(
-        jnp.broadcast_to(mine, (loaders, 4, head_size)), ("chip", "core"), split_axis=0, concat_axis=0, tiled=True
+        jnp.broadcast_to(mine, (loaders // 2, 4, head_size)), "chip", split_axis=0, concat_axis=0, tiled=True
     )
     gain_total = jnp.sum(every, axis=0).reshape(2, 2, head_size)
     return (gradients[:, None], gain_total)

time: 113 us -> 113 us (level)
  no operation moved by 1% of the time
where the time goes in v3:
time: 113 us
  blocking collectives  88.7 us (78%)
  starting transfers between devices  8.75 us (8%)
  Pallas kernels  8.62 us (8%)
  local copies, waits for them, and re-layouts  3.6 us (3%)
  other arithmetic  2.14 us (2%)
    all_to_all x1, blocking collectives, move_chunks(): lax.all_to_all(chunks, 'seq', split_axis=0, concat_axis=0, tiled=True)  32.8 us
    all_to_all x1, blocking collectives, move_rows(): return lax.all_to_all(rows, 'chip', split_axis=0, concat_axis=0, tiled=True)  25.8 us
    all_to_all x1, blocking collectives, shards(): lax.all_to_all(gain_parts.reshape(2 * bands, 4, head_size), ('core', 'seq...  21.1 us
    all_to_all x1, blocking collectives, shards(): lax.all_to_all(jnp.broadcast_to(mine, (loaders // 2, 4, head_size)), 'chi...  9.06 us
    ppermute x1, starting transfers between devices, shards(): other = lax.ppermute(other, 'core', [(0, 1), (1, 0)])  8.75 us
    pallas_call x1, Pallas kernels, shards(): gradients, gain_parts = attend(place, table, block_clip, arrived, chunks)  5.98 us
    unnamed x14, local copies, waits for them, and re-layouts  3.59 us
    pallas_call x2, Pallas kernels, gather(): pl.pallas_call(functools.partial(gather_kernel, flip, loaders, bands, cap...  2.52 us
  transfers between devices with their start and end apart: 1, of which 1 were waited for; matrix products, arithmetic and copies ran while one was open for 0% of the time, Pallas kernels for 1%

profile of v3, /device:TPU:1, one launch (start us, length us, event | category | flops | bytes accessed | tf_op | source)
XLA Modules:
  0.0 112.6 jit_solution(11959480120760949973)
XLA Ops:
  0.6 0.0 copy-start.6
  0.6 0.0 copy-start
  0.7 1.5 %copy-done = bf16[3,1,80,4096]{3,2,1,0:T(8,128)(2,1)S(1)} copy-done((bf16[3,1,80,4096]{3,2,1,0:T(8,128)(2,1)S(1)}, bf16[3,1,80,4096]{3,2,1,0:T(8,128)(2,1)}, u32[]{:S(2)}) %copy-start) | copy-done | bytes 1966104
  2.2 0.0 copy-start.2
  2.2 0.9 copy-done.2
  3.1 0.0 copy-start.1
  3.1 0.0 copy-start.3
  3.2 1.3 %gather_rows.1 = bf16[128,4608]{1,0:T(8,128)(2,1)S(1)} custom-call(s32[1]{0:T(128)} %bitcast.2.place_ref, s32[512,32]{1,0:T(8,128)S(1)} %bitcast.20, bf16[240,4096]{1,0:T(8,128)(2,1)S(1)} %bitcast.17), custom_call_target="tpu_custom_call" | custom-call | flops 300000000 | bytes 3000000 | tf_op jit(solution)/shard_map/gather_rows/pallas_call | solution.py:243
  4.4 8.7 %collective-permute-start = (bf16[128,4608]{1,0:T(8,128)(2,1)S(1)}, bf16[128,4608]{1,0:T(8,128)(2,1)}, u32[]{:S(2)}, u32[]{:S(2)}) collective-permute-start(bf16[128,4608]{1,0:T(8,128)(2,1)S(1)} %gather_rows.1), channel_id=1, source_target_pairs={{0,16},{16,0},{1,17},{17,1},{2,18},{18,2},{3,19},{19,3},{4,20},{20... | collective-permute-start | bytes 3538952 | tf_op jit(solution)/shard_map/ppermute | solution.py:268
  13.2 0.0 copy-done.6
  13.2 0.0 copy-start.4
  13.2 1.1 copy-done.4
  14.3 0.1 chunk_cotangent.1
  14.4 0.0 copy-done.1
  14.4 0.0 copy-done.3
  14.4 1.3 %gather_own.1 = bf16[128,4608]{1,0:T(8,128)(2,1)S(1)} custom-call(s32[1]{0:T(128)} %bitcast.2.place_ref, s32[512,32]{1,0:T(8,128)S(1)} %bitcast.21, bf16[240,4096]{1,0:T(8,128)(2,1)S(1)} %bitcast.18), custom_call_target="tpu_custom_call" | custom-call | flops 300000000 | bytes 3000000 | tf_op jit(solution)/shard_map/gather_own/pallas_call | solution.py:243
  15.7 0.1 collective-permute-done
  15.8 1.5 %pad_maximum_fusion = bf16[16,2,8,4608]{3,2,1,0:T(8,128)(2,1)S(1)} fusion(bf16[16,1,8,4608]{3,2,1,0:T(8,128)(2,1)} %bitcast.9, bf16[16,1,8,4608]{3,2,1,0:T(8,128)(2,1)S(1)} %bitcast.19), kind=kLoop, calls=%fused_computation | loop fusion | flops 1179648 | bytes 4718592 | tf_op jit(solution)/shard_map/concatenate | solution.py:271
  17.3 0.0 copy-start.5
  17.3 58.6 %conditional.1 = (bf16[16,168,128]{2,1,0:T(8,128)(2,1)S(1)}, bf16[256,4608]{1,0:T(8,128)(2,1)S(1)}) conditional(s32[]{:T(128)} %convert_element_type.3, (bf16[16,168,128]{2,1,0:T(8,128)(2,1)S(1)}, bf16[16,2,8,4608]{3,2,1,0:T(8,128)(2,1)S(1)}) %tuple.20, (bf16[16,2,8,4608]{3,2,1,0:T(8,128)(2,1)S(1)}, bf16[16,168,128]{2,1,0:T(8,128)(2,1)S(1)}) %tuple.21), branch_computations={%region_0.0_spmd, %region_1.0_spmd} | conditional | bytes 6094864 | solution.py:287
  17.3 32.8 %all_to_all.26 = bf16[16,168,128]{2,1,0:T(8,128)(2,1)S(1)} all-to-all(bf16[16,168,128]{2,1,0:T(8,128)(2,1)S(1)} %get-tuple-element.10), channel_id=1, replica_groups=mesh['chip'=16,'core'=2,'seq'=16] {'seq'}, dimensions={0} | all-to-all | bytes 1376256 | tf_op jit(solution)/shard_map/cond/branch_0_fun/all_to_all | solution.py:277
  50.0 25.8 %all_to_all.27 = bf16[16,2,8,4608]{3,2,1,0:T(8,128)(2,1)S(1)} all-to-all(bf16[16,2,8,4608]{3,2,1,0:T(8,128)(2,1)S(1)} %get-tuple-element.12), channel_id=1, replica_groups=mesh['chip'=16,'core'=2,'seq'=16] {'chip'}, dimensions={0} | all-to-all | bytes 4718592 | tf_op jit(solution)/shard_map/cond/branch_0_fun/all_to_all | solution.py:274
  75.8 0.0 copy-done.5
  75.8 6.0 %attend_pack.1 = (bf16[3,80,4096]{2,1,0:T(8,128)(2,1)}, f32[2,16,4,128]{3,2,1,0:T(4,128)S(1)}) custom-call(s32[1]{0:T(128)} %bitcast.2.place_ref, s32[512,32]{1,0:T(8,128)S(1)} %bitcast.22, s32[32,32]{1,0:T(8,128)S(1)} %copy-done.5, bf16[256,4608]{1,0:T(8,128)(2,1)S(1)} %get-tuple-element.23.rows_ref, bf16[16,168,128]{2,1,0:T(8,128)(2,1)S(1)} %get-tuple-element.24.chunk_ref), custom_call_target="tpu_custom_call" | custom-call | tf_op jit(solution)/shard_map/attend_pack/pallas_call | solution.py:316
  81.8 21.1 %all_to_all.30 = f32[32,4,128]{2,1,0:T(4,128)S(1)} all-to-all(f32[32,4,128]{2,1,0:T(4,128)S(1)} %bitcast.24), channel_id=1, replica_groups=mesh['chip'=16,'core'=2,'seq'=16] {'core','seq'}, dimensions={0} | all-to-all | bytes 131072 | tf_op jit(solution)/shard_map/all_to_all | solution.py:317
  102.9 9.1 %all_to_all.31 = f32[16,4,128]{2,1,0:T(4,128)S(1)} all-to-all(f32[16,4,128]{2,1,0:T(4,128)S(1)} %broadcast_in_dim.10), channel_id=1, replica_groups=mesh['chip'=16,'core'=2,'seq'=16] {'chip'}, dimensions={0} | all-to-all | bytes 65536 | tf_op jit(solution)/shard_map/all_to_all | solution.py:321
  112.0 0.6 reduce_sum.19
  (2 shorter events, 0.1 us)
Async XLA Ops:
  0.6 12.6 %copy-start.6 = (f32[2,2,128]{2,1,0:T(2,128)S(1)}, f32[2,2,128]{2,1,0:T(2,128)}, u32[]{:S(2)}) copy-start(f32[2,2,128]{2,1,0:T(2,128)} %gains_ref.1) | copy-start | bytes 6148
  0.6 1.5 %copy-start = (bf16[3,1,80,4096]{3,2,1,0:T(8,128)(2,1)S(1)}, bf16[3,1,80,4096]{3,2,1,0:T(8,128)(2,1)}, u32[]{:S(2)}) copy-start(bf16[3,1,80,4096]{3,2,1,0:T(8,128)(2,1)} %param.7) | copy-start | bytes 5898244
  2.2 0.9 copy-start.2
  3.1 11.3 %copy-start.1 = (bf16[3,1,80,4096]{3,2,1,0:T(8,128)(2,1)S(1)}, bf16[3,1,80,4096]{3,2,1,0:T(8,128)(2,1)}, u32[]{:S(2)}) copy-start(bf16[3,1,80,4096]{3,2,1,0:T(8,128)(2,1)} %param.7) | copy-start | bytes 5898244
  3.1 11.3 %copy-start.3 = (s32[32,16,32]{2,1,0:T(8,128)S(1)}, s32[32,16,32]{2,1,0:T(8,128)}, u32[]{:S(2)}) copy-start(s32[32,16,32]{2,1,0:T(8,128)} %param.10) | copy-start | bytes 196612
  4.4 11.3 %collective-permute-start = (bf16[128,4608]{1,0:T(8,128)(2,1)S(1)}, bf16[128,4608]{1,0:T(8,128)(2,1)}, u32[]{:S(2)}, u32[]{:S(2)}) collective-permute-start(bf16[128,4608]{1,0:T(8,128)(2,1)S(1)} %gather_rows.1), channel_id=1, source_target_pairs={{0,16},{16,0},{1,17},{17,1},{2,18},{18,2},{3,19},{19,3},{4,20},{20... | collective-permute-start | bytes 3538952 | tf_op jit(solution)/shard_map/ppermute | solution.py:268
  13.2 1.1 copy-start.4
  17.3 58.6 %copy-start.5 = (s32[32,32]{1,0:T(8,128)S(1)}, s32[32,32]{1,0:T(8,128)}, u32[]{:S(2)}) copy-start(s32[32,32]{1,0:T(8,128)} %clip_ref.1) | copy-start | bytes 12292
